TPU v7x, 128 devices: a whole 4x4x4 slice. The times are simulated.
128 devices in a mesh: wide: 16 (over z_hi, x, core), narrow: 8 (over z_lo, y).
Axes of the slice: x: 4, y: 4, z: 4 (z_hi: 2, z_lo: 2; z = z_hi * 2 + z_lo), core: 2. Of those that a mesh axis runs over, the one named last changes fastest.
Arguments:
- tokens: bfloat16 [12288, 1024], P(('wide', 'narrow')), may hold values from -6 to 6
- cotangent: bfloat16 [12288, 1024], P(('wide', 'narrow')), may hold values from -6 to 6
- segments: int32 [16, 768], P('wide'), may hold values from 0 to 3, never falling along the last dimension, each value on 1 to 384 neighbouring positions
- w_query: bfloat16 [1024, 1024], P(None, 'narrow'), may hold values from -0.1875 to 0.1875
- w_key: bfloat16 [1024, 1024], P(None, 'narrow'), may hold values from -0.1875 to 0.1875
- w_value: bfloat16 [1024, 1024], P(None, 'narrow'), may hold values from -0.1875 to 0.1875
- w_out: bfloat16 [1024, 1024], P('narrow'), may hold values from -1.5 to 1.5
- w_gate: bfloat16 [1024, 4096], P(None, 'narrow'), may hold values from -0.1875 to 0.1875
- w_up: bfloat16 [1024, 4096], P(None, 'narrow'), may hold values from -0.1875 to 0.1875
- w_down: bfloat16 [4096, 1024], P('narrow'), may hold values from -0.09375 to 0.09375
- gain_one: float32 [1024], replicated, may hold values from 0.25 to 1.75
- bias_one: float32 [1024], replicated, may hold values from -2.5 to 2.5
- gain_two: float32 [1024], replicated, may hold values from 0.25 to 1.75
- bias_two: float32 [1024], replicated, may hold values from -2.5 to 2.5
Outputs:
- layer_out: float32 [12288, 1024], P(('wide', 'narrow'))
- input_grad: float32 [12288, 1024], P(('wide', 'narrow'))
- grad_query: float32 [1024, 1024], P(None, 'narrow')
- grad_key: float32 [1024, 1024], P(None, 'narrow')
- grad_value: float32 [1024, 1024], P(None, 'narrow')
- grad_out: float32 [1024, 1024], P('narrow')
- grad_gate: float32 [1024, 4096], P(None, 'narrow')
- grad_up: float32 [1024, 4096], P(None, 'narrow')
- grad_down: float32 [4096, 1024], P('narrow')
- grad_gain_one: float32 [1024], replicated
- grad_bias_one: float32 [1024], replicated
- grad_gain_two: float32 [1024], replicated
- grad_bias_two: float32 [1024], replicated
Inputs may be any that keep to these rules, and one draw needn't show every extreme that they name: `segments`: within each row of 768 tokens segment numbers never fall; each segment holds 1 to 384 tokens and one holds exactly 384.
All inputs are finite; a program needn't handle non-finite values.
Results may differ from a plain program's by a relative error of at most 0.03.
Values may be sent and summed in bfloat16 or wider, within the bound.
No kernel may reach another device: no remote copies, remote signals or barrier semaphores. Data moves between devices by JAX's collectives and lax.ppermute only.
A program may use at most 128 MiB of HBM per device.

v0:
```python
import math
import jax
import jax.numpy as jnp
from jax import lax
from jax.sharding import PartitionSpec as P

HD = 64
EPS = 1e-05
MASKED = -1e30


def normalize(values, gain_vec, bias_vec):
    centred = values - jnp.mean(values, axis=-1, keepdims=True)
    inverse = lax.rsqrt(jnp.mean(centred * centred, axis=-1, keepdims=True) + EPS)
    scaled = centred * inverse
    return (scaled * gain_vec + bias_vec, scaled, inverse)


def normalize_back(grad_in, scaled, inverse, gain_vec):
    along = grad_in * gain_vec
    return inverse * (
        along
        - jnp.mean(along, axis=-1, keepdims=True)
        - scaled * jnp.mean(along * scaled, axis=-1, keepdims=True)
    )


def contract_last(left_side, right_side):
    return lax.dot_general(
        left_side, right_side, (((1,), (1,)), ((), ())), preferred_element_type=jnp.float32
    )


def contract_first(left_side, right_side):
    return lax.dot_general(
        left_side, right_side, (((0,), (0,)), ((), ())), preferred_element_type=jnp.float32
    )


def rotary_tables(seg_rows):
    length = seg_rows.shape[-1]
    column = lax.broadcasted_iota(jnp.int32, (length, length), 1)
    row_index = lax.broadcasted_iota(jnp.int32, (length,), 0)
    same_segment = seg_rows[..., :, None] == seg_rows[..., None, :]
    first_index = jnp.min(jnp.where(same_segment, column, length), axis=-1)
    position = (row_index - first_index).astype(jnp.float32)
    half_width = HD // 2
    inverse = 10000.0 ** (-(2.0 * jnp.arange(half_width).astype(jnp.float32) / HD))
    angles = position[..., None] * inverse
    return (jnp.cos(angles), jnp.sin(angles), same_segment)


def rotate(values, cosine_table, sine_table):
    half_width = values.shape[-1] // 2
    first_half = values[..., :half_width]
    second_half = values[..., half_width:]
    cosine = cosine_table[..., None, :]
    sine_part = sine_table[..., None, :]
    return jnp.concatenate(
        [
            first_half * cosine - second_half * sine_part,
            second_half * cosine + first_half * sine_part,
        ],
        axis=-1,
    )


def unrotate(values, cosine_table, sine_table):
    half_width = values.shape[-1] // 2
    first_half = values[..., :half_width]
    second_half = values[..., half_width:]
    cosine = cosine_table[..., None, :]
    sine_part = sine_table[..., None, :]
    return jnp.concatenate(
        [
            first_half * cosine + second_half * sine_part,
            second_half * cosine - first_half * sine_part,
        ],
        axis=-1,
    )


def project_heads(normed_one, w_query, w_key, w_value, cosine_table, sine_table):
    row_count, length = (cosine_table.shape[0], cosine_table.shape[1])
    head_shape = (row_count, length, w_query.shape[1] // HD, HD)
    queries = rotate(
        jnp.dot(normed_one, w_query, preferred_element_type=jnp.float32).reshape(head_shape),
        cosine_table,
        sine_table,
    ).astype(jnp.bfloat16)
    key_rows = rotate(
        jnp.dot(normed_one, w_key, preferred_element_type=jnp.float32).reshape(head_shape),
        cosine_table,
        sine_table,
    ).astype(jnp.bfloat16)
    value_rows = (
        jnp.dot(normed_one, w_value, preferred_element_type=jnp.float32)
        .astype(jnp.bfloat16)
        .reshape(head_shape)
    )
    return (queries, key_rows, value_rows)


def attention_forward(normed_one, w_query, w_key, w_value, cosine_table, sine_table, same_segment):
    queries, key_rows, value_rows = project_heads(
        normed_one, w_query, w_key, w_value, cosine_table, sine_table
    )
    score_scale = 1.0 / math.sqrt(HD)

    def one_row(row_items):
        query_row, key_row, value_row, mask_row = row_items
        scores = (
            jnp.einsum("qhd,khd->hqk", query_row, key_row, preferred_element_type=jnp.float32)
            * score_scale
        )
        scores = jnp.where(mask_row[None], scores, MASKED)
        row_peak = jnp.max(scores, axis=-1, keepdims=True)
        exponent = jnp.exp(scores - row_peak)
        row_total = jnp.sum(exponent, axis=-1, keepdims=True)
        probs_low = (exponent / row_total).astype(jnp.bfloat16)
        output = jnp.einsum(
            "hqk,khd->qhd", probs_low, value_row, preferred_element_type=jnp.float32
        ).astype(jnp.bfloat16)
        return (output, row_peak + jnp.log(row_total))

    attended, log_total = lax.map(one_row, (queries, key_rows, value_rows, same_segment))
    return (attended.reshape(normed_one.shape[0], -1), log_total)


def attention_grads(
    normed_one,
    attended,
    log_total,
    branch_grad,
    w_query,
    w_key,
    w_value,
    w_out,
    cosine_table,
    sine_table,
    same_segment,
):
    queries, key_rows, value_rows = project_heads(
        normed_one, w_query, w_key, w_value, cosine_table, sine_table
    )
    score_scale = 1.0 / math.sqrt(HD)
    grad_out = contract_first(attended, branch_grad)
    attended_grad = contract_last(branch_grad, w_out).astype(jnp.bfloat16).reshape(queries.shape)

    def one_row(row_items):
        query_row, key_row, value_row, mask_row, total_row, grad_row = row_items
        scores = (
            jnp.einsum("qhd,khd->hqk", query_row, key_row, preferred_element_type=jnp.float32)
            * score_scale
        )
        scores = jnp.where(mask_row[None], scores, MASKED)
        probs = jnp.exp(scores - total_row)
        probs_low = probs.astype(jnp.bfloat16)
        prob_grad = jnp.einsum(
            "qhd,khd->hqk", grad_row, value_row, preferred_element_type=jnp.float32
        )
        score_grad = (
            probs * (prob_grad - jnp.sum(probs * prob_grad, axis=-1, keepdims=True))
        ).astype(jnp.bfloat16)
        query_grad = score_scale * jnp.einsum(
            "hqk,khd->qhd", score_grad, key_row, preferred_element_type=jnp.float32
        )
        key_grad = score_scale * jnp.einsum(
            "hqk,qhd->khd", score_grad, query_row, preferred_element_type=jnp.float32
        )
        value_grad = jnp.einsum(
            "hqk,qhd->khd", probs_low, grad_row, preferred_element_type=jnp.float32
        ).astype(jnp.bfloat16)
        return (query_grad, key_grad, value_grad)

    query_grad, key_grad, value_grad = lax.map(
        one_row, (queries, key_rows, value_rows, same_segment, log_total, attended_grad)
    )
    token_count = normed_one.shape[0]
    query_grad = (
        unrotate(query_grad, cosine_table, sine_table).astype(jnp.bfloat16).reshape(token_count, -1)
    )
    key_grad = (
        unrotate(key_grad, cosine_table, sine_table).astype(jnp.bfloat16).reshape(token_count, -1)
    )
    value_grad = value_grad.reshape(token_count, -1)
    grad_query = contract_first(normed_one, query_grad)
    grad_key = contract_first(normed_one, key_grad)
    grad_value = contract_first(normed_one, value_grad)
    partial_sum = (
        contract_last(query_grad, w_query)
        + contract_last(key_grad, w_key)
        + contract_last(value_grad, w_value)
    )
    return (partial_sum, grad_query, grad_key, grad_value, grad_out)


def swiglu(normed_two, w_gate, w_up):
    gate_pre = jnp.dot(normed_two, w_gate, preferred_element_type=jnp.float32)
    up_pre = jnp.dot(normed_two, w_up, preferred_element_type=jnp.float32)
    sigmoid_gate = jax.nn.sigmoid(gate_pre)
    active = gate_pre * sigmoid_gate
    hidden = (active * up_pre).astype(jnp.bfloat16)
    return (hidden, gate_pre, up_pre, sigmoid_gate, active)


def swiglu_grads(normed_two, out_grad, w_gate, w_up, w_down):
    hidden, gate_pre, up_pre, sigmoid_gate, active = swiglu(normed_two, w_gate, w_up)
    hidden_grad = contract_last(out_grad, w_down)
    grad_down = contract_first(hidden, out_grad)
    gate_grad = (
        hidden_grad * up_pre * sigmoid_gate * (1.0 + gate_pre * (1.0 - sigmoid_gate))
    ).astype(jnp.bfloat16)
    up_grad = (hidden_grad * active).astype(jnp.bfloat16)
    grad_gate = contract_first(normed_two, gate_grad)
    grad_up = contract_first(normed_two, up_grad)
    partial_sum = contract_last(gate_grad, w_gate) + contract_last(up_grad, w_up)
    return (partial_sum, grad_gate, grad_up, grad_down)


def per_device(
    tokens,
    cotangent,
    segments,
    w_query,
    w_key,
    w_value,
    w_out,
    w_gate,
    w_up,
    w_down,
    gain_one,
    bias_one,
    gain_two,
    bias_two,
):
    shard_rows = tokens.shape[0]
    narrow_index = lax.axis_index("narrow")
    cosine_table, sine_table, same_segment = rotary_tables(segments)
    gathered, cot_whole = (
        lax.all_gather(tokens, "narrow", axis=0, tiled=True),
        lax.all_gather(cotangent, "narrow", axis=0, tiled=True),
    )
    inputs = gathered.astype(jnp.float32)
    normed_float, scaled_one, inverse_one = normalize(inputs, gain_one, bias_one)
    normed_one = normed_float.astype(jnp.bfloat16)
    attended, log_total = attention_forward(
        normed_one, w_query, w_key, w_value, cosine_table, sine_table, same_segment
    )
    middle = inputs + lax.psum(
        jnp.dot(attended, w_out, preferred_element_type=jnp.float32).astype(jnp.bfloat16), "narrow"
    ).astype(jnp.float32)
    normed_float_two, scaled_two, inverse_two = normalize(middle, gain_two, bias_two)
    normed_two = normed_float_two.astype(jnp.bfloat16)
    hidden = swiglu(normed_two, w_gate, w_up)[0]
    result_whole = middle + lax.psum(
        jnp.dot(hidden, w_down, preferred_element_type=jnp.float32).astype(jnp.bfloat16), "narrow"
    ).astype(jnp.float32)
    layer_out = lax.dynamic_slice_in_dim(result_whole, narrow_index * shard_rows, shard_rows, 0)
    partial_two, grad_gate, grad_up, grad_down = swiglu_grads(
        normed_two, cot_whole, w_gate, w_up, w_down
    )
    normed_two_grad = lax.psum(partial_two.astype(jnp.bfloat16), "narrow").astype(jnp.float32)
    middle_grad = cot_whole.astype(jnp.float32) + normalize_back(
        normed_two_grad, scaled_two, inverse_two, gain_two
    )
    own_two_grad = lax.dynamic_slice_in_dim(
        normed_two_grad, narrow_index * shard_rows, shard_rows, 0
    )
    own_scaled_two = lax.dynamic_slice_in_dim(scaled_two, narrow_index * shard_rows, shard_rows, 0)
    branch_grad = middle_grad.astype(jnp.bfloat16)
    partial_one, grad_query, grad_key, grad_value, grad_out = attention_grads(
        normed_one,
        attended,
        log_total,
        branch_grad,
        w_query,
        w_key,
        w_value,
        w_out,
        cosine_table,
        sine_table,
        same_segment,
    )
    normed_one_grad = lax.psum(partial_one.astype(jnp.bfloat16), "narrow").astype(jnp.float32)
    input_whole = middle_grad + normalize_back(normed_one_grad, scaled_one, inverse_one, gain_one)
    input_grad = lax.dynamic_slice_in_dim(input_whole, narrow_index * shard_rows, shard_rows, 0)
    own_one_grad = lax.dynamic_slice_in_dim(
        normed_one_grad, narrow_index * shard_rows, shard_rows, 0
    )
    own_scaled_one = lax.dynamic_slice_in_dim(scaled_one, narrow_index * shard_rows, shard_rows, 0)
    matrices = (
        lax.psum(grad_query.astype(jnp.bfloat16), "wide").astype(jnp.float32),
        lax.psum(grad_key.astype(jnp.bfloat16), "wide").astype(jnp.float32),
        lax.psum(grad_value.astype(jnp.bfloat16), "wide").astype(jnp.float32),
        lax.psum(grad_out.astype(jnp.bfloat16), "wide").astype(jnp.float32),
        lax.psum(grad_gate.astype(jnp.bfloat16), "wide").astype(jnp.float32),
        lax.psum(grad_up.astype(jnp.bfloat16), "wide").astype(jnp.float32),
        lax.psum(grad_down.astype(jnp.bfloat16), "wide").astype(jnp.float32),
    )
    norm_grads = lax.psum(
        (
            jnp.sum(own_one_grad * own_scaled_one, axis=0),
            jnp.sum(own_one_grad, axis=0),
            jnp.sum(own_two_grad * own_scaled_two, axis=0),
            jnp.sum(own_two_grad, axis=0),
        ),
        ("wide", "narrow"),
    )
    return (
        layer_out,
        input_grad,
        matrices[0],
        matrices[1],
        matrices[2],
        matrices[3],
        matrices[4],
        matrices[5],
        matrices[6],
        norm_grads[0],
        norm_grads[1],
        norm_grads[2],
        norm_grads[3],
    )


def solution(mesh):
    placed = (
        P(("wide", "narrow"), None),
        P(("wide", "narrow"), None),
        P("wide", None),
        P(None, "narrow"),
        P(None, "narrow"),
        P(None, "narrow"),
        P("narrow", None),
        P(None, "narrow"),
        P(None, "narrow"),
        P("narrow", None),
        P(),
        P(),
        P(),
        P(),
    )
    return jax.shard_map(
        per_device,
        mesh=mesh,
        in_specs=placed,
        out_specs=(
            P(("wide", "narrow"), None),
            P(("wide", "narrow"), None),
            P(None, "narrow"),
            P(None, "narrow"),
            P(None, "narrow"),
            P("narrow", None),
            P(None, "narrow"),
            P(None, "narrow"),
            P("narrow", None),
            P(),
            P(),
            P(),
            P(),
        ),
        check_vma=False,
    )
```

profile of v0, /device:TPU:0, one launch (start us, length us, event | category | flops | bytes accessed | tf_op | source)
XLA Modules:
  0.0 550.6 jit_solution(14009956408082012891)
XLA Ops:
  10.9 41.9 %all-gather.3.cloned.1.call-done = bf16[768,1024]{1,0:T(8,128)(2,1)} async-done(((bf16[96,1024]{1,0:T(8,128)(2,1)}), bf16[768,1024]{1,0:T(8,128)(2,1)}) %all-gather.3.cloned.1.call-update) | async-done | bytes 1572880 | tf_op jit(solution)/shard_map/all_gather | solution.py:241
  52.8 1.8 convert_reduce_fusion
  54.6 2.0 fusion.4
  63.5 1.7 convolution_convert_fusion.1
  66.2 77.9 %all-reduce.8.cloned.1.call-done = bf16[768,1024]{1,0:T(8,128)(2,1)} async-done(((bf16[768,1024]{1,0:T(8,128)(2,1)}), bf16[768,1024]{1,0:T(8,128)(2,1)}) %all-reduce.8.cloned.1.call-update) | async-done | bytes 1572880 | tf_op jit(solution)/shard_map/psum | solution.py:250
  144.1 2.0 fusion.28
  146.9 3.6 add_convert_fusion.2
  150.4 2.1 fusion.32
  152.6 2.1 fusion.33
  154.7 31.3 %all-gather.5.cloned.1.call-done = bf16[768,1024]{1,0:T(8,128)(2,1)} async-done(((bf16[96,1024]{1,0:T(8,128)(2,1)}), bf16[768,1024]{1,0:T(8,128)(2,1)}) %all-gather.5.cloned.1.call-update) | async-done | bytes 1572880 | tf_op jit(solution)/shard_map/all_gather | solution.py:242
  185.9 5.0 multiply_convert_fusion.1
  192.7 2.2 add_convert_fusion.1
  195.2 3.3 convolution_convert_fusion
  198.4 75.3 %all-reduce.10.cloned.1.call-done = bf16[768,1024]{1,0:T(8,128)(2,1)} async-done(((bf16[768,1024]{1,0:T(8,128)(2,1)}), bf16[768,1024]{1,0:T(8,128)(2,1)}) %all-reduce.10.cloned.1.call-update) | async-done | bytes 1572880 | tf_op jit(solution)/shard_map/psum | solution.py:263
  273.7 3.2 multiply_reduce_fusion.4
  277.5 2.6 multiply_add_fusion
  286.7 1.8 add_convert_fusion
  288.8 3.7 convolution_convert_fusion.3
  292.6 2.0 convolution_convert_fusion.4
  294.6 2.0 convolution_convert_fusion.2
  296.6 1.3 convolution_convert_fusion.6
  297.9 1.3 convolution_convert_fusion.7
  301.8 3.4 convert_element_type.182
  305.2 73.7 %all-reduce.14.cloned.1.call-done = (bf16[768,1024]{1,0:T(8,128)(2,1)}, bf16[768,1024]{1,0:T(8,128)(2,1)}) async-done(((bf16[768,1024]{1,0:T(8,128)(2,1)}, bf16[768,1024]{1,0:T(8,128)(2,1)}), (bf16[768,1024]{1,0:T(8,128)(2,1)}, bf16[768,1024]{1,0:T(8,128)(2,1)})) %all-reduce.14.cloned.1.call-update) | async-done | bytes 3145744 | tf_op jit(solution)/shard_map/psum | solution.py:256
  378.9 1.9 convert_element_type.192
  382.2 2.2 dynamic-slice_reduce_fusion
  384.4 65.4 %all-reduce = (f32[1024]{0:T(1024)}, f32[1024]{0:T(1024)}, f32[1024]{0:T(1024)}, f32[1024]{0:T(1024)}) all-reduce(f32[1024]{0:T(1024)S(1)} %get-tuple-element.113, f32[1024]{0:T(1024)S(1)} %get-tuple-element.114, f32[1024]{0:T(1024)S(1)} %get-tuple-element.55, ...), channel_id=1, replica_groups=mesh['wide'=16,'narrow'=8] {'wide','narrow'}, use_global_device_ids=true, to_apply=%region_24.25 | all-reduce | flops 4096 | bytes 32768 | tf_op jit(solution)/shard_map/psum | solution.py:301
  449.8 1.8 dynamic-slice_add_fusion.1
  451.6 82.6 %all-reduce.12.cloned.1.call-done = (bf16[1024,128]{1,0:T(8,128)(2,1)}, bf16[1024,128]{1,0:T(8,128)(2,1)}, bf16[1024,128]{1,0:T(8,128)(2,1)}, bf16[128,1024]{1,0...) async-done(((bf16[1024,128]{1,0:T(8,128)(2,1)}, bf16[1024,128]{1,0:T(8,128)(2,1)}, bf16[1024,128]{1,0:T(8,128)(2,1)}, ...) | async-done | bytes 4194320 | tf_op jit(solution)/shard_map/psum | solution.py:293
  534.2 3.0 convert_element_type.202
  537.2 1.6 convert_element_type.204
  538.8 1.6 convert_element_type.206
  (169 shorter events, 28.7 us)
Async XLA Ops:
  7.2 178.8 %copy-start = (bf16[512,1024]{1,0:T(8,128)(2,1)S(1)}, bf16[512,1024]{1,0:T(8,128)(2,1)}, u32[]{:S(2)}) copy-start(bf16[512,1024]{1,0:T(8,128)(2,1)} %param.23) | copy-start | bytes 3145732
  7.2 49.4 %copy-start.49 = (f32[1024]{0:T(1024)S(1)}, f32[1024]{0:T(1024)}, u32[]{:S(2)}) copy-start(f32[1024]{0:T(1024)} %param.24) | copy-start | bytes 12292
  7.2 49.4 %copy-start.50 = (f32[1024]{0:T(1024)S(1)}, f32[1024]{0:T(1024)}, u32[]{:S(2)}) copy-start(f32[1024]{0:T(1024)} %param.25) | copy-start | bytes 12292
  7.2 45.6 %all-gather.3.cloned.1.call-start = ((), (), s32[]{:S(2)}) async-start(), calls=%async_computation | async-start | bytes 1769472 | tf_op jit(solution)/shard_map/all_gather | solution.py:241
  8.0 136.2 %all-reduce.8.cloned.1.call-start = ((), (), s32[]{:S(2)}) async-start(), calls=%async_computation.1 | async-start | bytes 3145728 | tf_op jit(solution)/shard_map/psum | solution.py:250
  9.7 49.7 %copy-start.26 = (f32[768,32]{0,1:T(8,128)}, f32[768,32]{0,1:T(8,128)S(1)}, u32[]{:S(2)}) copy-start(f32[768,32]{0,1:T(8,128)S(1)} %get-tuple-element.107) | copy-start | bytes 294916
  10.9 46.4 %copy-start.22 = (bf16[1024,128]{1,0:T(8,128)(2,1)S(1)}, bf16[1024,128]{1,0:T(8,128)(2,1)}, u32[]{:S(2)}) copy-start(bf16[1024,128]{1,0:T(8,128)(2,1)} %param.17) | copy-start | bytes 786436
  52.8 3.9 copy-start.2
  54.6 3.4 copy-start.21
  65.2 120.7 %all-gather.5.cloned.1.call-start = ((), (), s32[]{:S(2)}) async-start(), calls=%async_computation.2 | async-start | bytes 1769472 | tf_op jit(solution)/shard_map/all_gather | solution.py:242
  66.0 80.9 %copy-start.48 = (f32[1024]{0:T(1024)S(1)}, f32[1024]{0:T(1024)}, u32[]{:S(2)}) copy-start(f32[1024]{0:T(1024)} %param.26) | copy-start | bytes 12292
  66.0 80.9 %copy-start.51 = (f32[1024]{0:T(1024)S(1)}, f32[1024]{0:T(1024)}, u32[]{:S(2)}) copy-start(f32[1024]{0:T(1024)} %param.27) | copy-start | bytes 12292
  66.0 207.7 %all-reduce.10.cloned.1.call-start = ((), (), s32[]{:S(2)}) async-start(), calls=%async_computation.3 | async-start | bytes 3145728 | tf_op jit(solution)/shard_map/psum | solution.py:263
  146.9 3.6 copy-start.15
  185.9 5.0 copy-start.16
  194.9 184.0 %all-reduce.14.cloned.1.call-start = ((), (), s32[]{:S(2)}) async-start(), calls=%async_computation.5 | async-start | bytes 6291456 | tf_op jit(solution)/shard_map/psum | solution.py:256
  273.7 3.3 copy-start.8
  273.7 3.8 copy-start.9
  273.7 7.0 %slice-start = ((s8[4718592]{0:T(1024)(128)(4,1)}), s8[4194304]{0:T(1024)(128)(4,1)S(1)}, s32[]{:S(2)}) async-start(s8[4718592]{0:T(1024)(128)(4,1)} %bitcast.74), calls=%async_computation.6 | async-start | bytes 8388608
  277.5 3.3 slice-start.1
  288.5 4.1 copy-start.29
  288.5 245.7 %all-reduce.12.cloned.1.call-start = ((), (), s32[]{:S(2)}) async-start(), calls=%async_computation.4 | async-start | bytes 8388608 | tf_op jit(solution)/shard_map/psum | solution.py:293
  288.8 3.7 copy-start.14
  296.6 4.0 copy-start.7
  296.6 4.0 copy-start.32
  534.2 3.0 copy-start.20
  534.2 4.6 copy-start.19
  537.2 3.2 copy-start.47
  537.2 4.0 copy-start.46
  538.8 3.2 copy-start.45
  538.8 4.1 copy-start.44
  538.8 4.9 copy-start.1
  (29 other events, 46.5 us)
Sparse Core Ops, SparseCore 0:
  9.7 43.0 all-gather.2
  65.4 78.7 all-reduce.7
  145.8 40.1 all-gather.4
  195.0 78.6 all-reduce.9
  288.6 90.2 all-reduce.13
  382.4 151.7 all-reduce.11
where the time goes:
time: 551 us
  waiting for transfers between devices  384 us (70%)
  blocking collectives  65.4 us (12%)
  other arithmetic  41.2 us (7%)
  matrix products  41 us (7%)
  between operations  14.8 us (3%)
    psum x1, waiting for transfers between devices, per_device(): lax.psum(grad_query.astype(jnp.bfloat16), 'wide').astype(jnp.float32)  82.6 us
    psum x1, waiting for transfers between devices, per_device(): lax.psum(jnp.dot(attended, w_out, preferred_element_type=jnp.float32).ast...  77.9 us
    psum x1, waiting for transfers between devices, per_device(): lax.psum(partial_two.astype(jnp.bfloat16), 'narrow').astype(jnp.float32)  75.3 us
    psum x1, waiting for transfers between devices, per_device(): lax.psum(jnp.dot(hidden, w_down, preferred_element_type=jnp.float32).asty...  73.7 us
    psum x1, blocking collectives, per_device(): lax.psum((jnp.sum(own_one_grad * own_scaled_one, axis=0), jnp.sum(own_one...  65.4 us
    all_gather x1, waiting for transfers between devices, per_device(): lax.all_gather(tokens, 'narrow', axis=0, tiled=True)  41.9 us
    all_gather x1, waiting for transfers between devices, per_device(): lax.all_gather(cotangent, 'narrow', axis=0, tiled=True)  31.3 us
    dot_general x7, matrix products, contract_first(): lax.dot_general(left_side, right_side, (((0,), (0,)), ((), ())), preferre...  12.8 us
  transfers between devices with their start and end apart: 6, of which 6 were waited for; matrix products, arithmetic and copies ran while one was open for 7% of the time, Pallas kernels for 0%

commit v1 on v0

--- a/solution.py
+++ b/solution.py
@@ -239,7 +239,9 @@
     cosine_table, sine_table, same_segment = rotary_tables(segments)
     gathered, cot_whole = (
         lax.all_gather(tokens, "narrow", axis=0, tiled=True),
-        lax.all_gather(cotangent, "narrow", axis=0, tiled=True),
+        jnp.concatenate(
+            lax.all_to_all(jnp.stack([cotangent] * lax.axis_size("narrow")), "narrow", 0, 0), axis=0
+        ),
     )
     inputs = gathered.astype(jnp.float32)
     normed_float, scaled_one, inverse_one = normalize(inputs, gain_one, bias_one)

time: 551 us -> 528 us (0.958)
  waiting for transfers between devices: 384 us -> 353 us
    all_gather x1 -> x0, waiting for transfers between devices: 31.3 us -> none  [per_device(): lax.all_gather(cotangent, 'narrow', axis=0, tiled=True)]
  transfers between devices with their start and end apart: 6 -> 6, of which waited for: 6 -> 5; matrix products, arithmetic and copies ran while one was open for 7% -> 8% of each run, Pallas kernels for 0% -> 0%
where the time goes in v1:
time: 528 us
  waiting for transfers between devices  353 us (67%)
  blocking collectives  65.4 us (12%)
  matrix products  42.5 us (8%)
  other arithmetic  41.2 us (8%)
  between operations  14.5 us (3%)
  local copies, waits for them, and re-layouts  5.51 us (1%)
    psum x1, waiting for transfers between devices, per_device(): lax.psum(grad_query.astype(jnp.bfloat16), 'wide').astype(jnp.float32)  82.6 us
    psum x1, waiting for transfers between devices, per_device(): lax.psum(jnp.dot(attended, w_out, preferred_element_type=jnp.float32).ast...  80.2 us
    psum x1, waiting for transfers between devices, per_device(): lax.psum(partial_two.astype(jnp.bfloat16), 'narrow').astype(jnp.float32)  75.8 us
    psum x1, waiting for transfers between devices, per_device(): lax.psum(jnp.dot(hidden, w_down, preferred_element_type=jnp.float32).asty...  72.2 us
    psum x1, blocking collectives, per_device(): lax.psum((jnp.sum(own_one_grad * own_scaled_one, axis=0), jnp.sum(own_one...  65.4 us
    all_gather x1, waiting for transfers between devices, per_device(): lax.all_gather(tokens, 'narrow', axis=0, tiled=True)  41.9 us
    dot_general x7, matrix products, contract_first(): lax.dot_general(left_side, right_side, (((0,), (0,)), ((), ())), preferre...  14.3 us
    dot_general x7, matrix products, contract_last(): lax.dot_general(left_side, right_side, (((1,), (1,)), ((), ())), preferre...  11.8 us
  transfers between devices with their start and end apart: 6, of which 5 were waited for; matrix products, arithmetic and copies ran while one was open for 8% of the time, Pallas kernels for 0%

profile of v1, /device:TPU:0, one launch (start us, length us, event | category | flops | bytes accessed | tf_op | source)
XLA Modules:
  0.0 527.7 jit_solution(1537145044844240489)
XLA Ops:
  10.9 41.9 %all-gather.2.cloned.1.call-done = bf16[768,1024]{1,0:T(8,128)(2,1)} async-done(((bf16[96,1024]{1,0:T(8,128)(2,1)}), bf16[768,1024]{1,0:T(8,128)(2,1)}) %all-gather.2.cloned.1.call-update) | async-done | bytes 1572880 | tf_op jit(solution)/shard_map/all_gather | solution.py:241
  52.8 1.8 convert_reduce_fusion
  54.6 2.0 fusion.4
  63.5 1.7 convolution_convert_fusion.1
  65.2 2.3 stack.2
  67.5 4.3 all-to-all-start
  72.1 80.2 %all-reduce.8.cloned.1.call-done = bf16[768,1024]{1,0:T(8,128)(2,1)} async-done(((bf16[768,1024]{1,0:T(8,128)(2,1)}), bf16[768,1024]{1,0:T(8,128)(2,1)}) %all-reduce.8.cloned.1.call-update) | async-done | bytes 1572880 | tf_op jit(solution)/shard_map/psum | solution.py:252
  152.3 2.0 fusion.28
  155.0 3.5 add_convert_fusion.2
  158.6 2.1 fusion.32
  160.7 2.1 fusion.33
  162.8 5.0 multiply_convert_fusion.1
  169.6 2.2 add_convert_fusion.1
  172.1 3.3 convolution_convert_fusion
  175.3 75.8 %all-reduce.10.cloned.1.call-done = bf16[768,1024]{1,0:T(8,128)(2,1)} async-done(((bf16[768,1024]{1,0:T(8,128)(2,1)}), bf16[768,1024]{1,0:T(8,128)(2,1)}) %all-reduce.10.cloned.1.call-update) | async-done | bytes 1572880 | tf_op jit(solution)/shard_map/psum | solution.py:265
  251.2 3.2 multiply_reduce_fusion.4
  254.9 2.6 multiply_add_fusion
  264.2 1.8 add_convert_fusion
  266.3 3.7 convolution_convert_fusion.3
  270.0 2.0 convolution_convert_fusion.4
  272.0 3.5 convolution_convert_fusion.2
  275.5 1.3 convolution_convert_fusion.6
  280.7 3.5 convert_element_type.182
  284.2 72.2 %all-reduce.14.cloned.1.call-done = (bf16[768,1024]{1,0:T(8,128)(2,1)}, bf16[768,1024]{1,0:T(8,128)(2,1)}) async-done(((bf16[768,1024]{1,0:T(8,128)(2,1)}, bf16[768,1024]{1,0:T(8,128)(2,1)}), (bf16[768,1024]{1,0:T(8,128)(2,1)}, bf16[768,1024]{1,0:T(8,128)(2,1)})) %all-reduce.14.cloned.1.call-update) | async-done | bytes 3145744 | tf_op jit(solution)/shard_map/psum | solution.py:258
  356.3 1.9 convert_element_type.192
  359.6 2.2 dynamic-slice_reduce_fusion
  361.8 65.4 %all-reduce = (f32[1024]{0:T(1024)}, f32[1024]{0:T(1024)}, f32[1024]{0:T(1024)}, f32[1024]{0:T(1024)}) all-reduce(f32[1024]{0:T(1024)S(1)} %get-tuple-element.113, f32[1024]{0:T(1024)S(1)} %get-tuple-element.114, f32[1024]{0:T(1024)S(1)} %get-tuple-element.55, ...), channel_id=1, replica_groups=mesh['wide'=16,'narrow'=8] {'wide','narrow'}, use_global_device_ids=true, to_apply=%region_24.25 | all-reduce | flops 4096 | bytes 32768 | tf_op jit(solution)/shard_map/psum | solution.py:303
  427.2 1.8 dynamic-slice_add_fusion.1
  429.0 82.6 %all-reduce.12.cloned.1.call-done = (bf16[1024,128]{1,0:T(8,128)(2,1)}, bf16[1024,128]{1,0:T(8,128)(2,1)}, bf16[1024,128]{1,0:T(8,128)(2,1)}, bf16[128,1024]{1,0...) async-done(((bf16[1024,128]{1,0:T(8,128)(2,1)}, bf16[1024,128]{1,0:T(8,128)(2,1)}, bf16[1024,128]{1,0:T(8,128)(2,1)}, ...) | async-done | bytes 4194320 | tf_op jit(solution)/shard_map/psum | solution.py:295
  511.6 3.0 convert_element_type.202
  514.6 1.6 convert_element_type.204
  516.2 1.6 convert_element_type.206
  (167 shorter events, 29.3 us)
Async XLA Ops:
  7.2 155.7 %copy-start = (bf16[512,1024]{1,0:T(8,128)(2,1)S(1)}, bf16[512,1024]{1,0:T(8,128)(2,1)}, u32[]{:S(2)}) copy-start(bf16[512,1024]{1,0:T(8,128)(2,1)} %param.23) | copy-start | bytes 3145732
  7.2 49.4 %copy-start.48 = (f32[1024]{0:T(1024)S(1)}, f32[1024]{0:T(1024)}, u32[]{:S(2)}) copy-start(f32[1024]{0:T(1024)} %param.24) | copy-start | bytes 12292
  7.2 49.4 %copy-start.49 = (f32[1024]{0:T(1024)S(1)}, f32[1024]{0:T(1024)}, u32[]{:S(2)}) copy-start(f32[1024]{0:T(1024)} %param.25) | copy-start | bytes 12292
  7.2 45.6 %all-gather.2.cloned.1.call-start = ((), (), s32[]{:S(2)}) async-start(), calls=%async_computation.1 | async-start | bytes 1769472 | tf_op jit(solution)/shard_map/all_gather | solution.py:241
  8.0 144.3 %all-reduce.8.cloned.1.call-start = ((), (), s32[]{:S(2)}) async-start(), calls=%async_computation.2 | async-start | bytes 3145728 | tf_op jit(solution)/shard_map/psum | solution.py:252
  9.7 49.7 %copy-start.25 = (f32[768,32]{0,1:T(8,128)}, f32[768,32]{0,1:T(8,128)S(1)}, u32[]{:S(2)}) copy-start(f32[768,32]{0,1:T(8,128)S(1)} %get-tuple-element.107) | copy-start | bytes 294916
  10.9 46.4 %copy-start.21 = (bf16[1024,128]{1,0:T(8,128)(2,1)S(1)}, bf16[1024,128]{1,0:T(8,128)(2,1)}, u32[]{:S(2)}) copy-start(bf16[1024,128]{1,0:T(8,128)(2,1)} %param.17) | copy-start | bytes 786436
  52.8 3.9 copy-start.2
  54.6 3.4 copy-start.20
  67.5 95.3 %all-to-all-start = ((bf16[8,96,1024]{2,1,0:T(8,128)(2,1)}), bf16[8,96,1024]{2,1,0:T(8,128)(2,1)}, u32[]{:S(2)}, u32[]{:S(2)}) async-start(bf16[8,96,1024]{2,1,0:T(8,128)(2,1)} %stack.2), calls=%async_computation | async-start | bytes 3145728 | tf_op jit(solution)/shard_map/all_to_all | solution.py:243
  71.8 83.2 %copy-start.47 = (f32[1024]{0:T(1024)S(1)}, f32[1024]{0:T(1024)}, u32[]{:S(2)}) copy-start(f32[1024]{0:T(1024)} %param.26) | copy-start | bytes 12292
  71.8 83.2 %copy-start.50 = (f32[1024]{0:T(1024)S(1)}, f32[1024]{0:T(1024)}, u32[]{:S(2)}) copy-start(f32[1024]{0:T(1024)} %param.27) | copy-start | bytes 12292
  71.8 179.3 %all-reduce.10.cloned.1.call-start = ((), (), s32[]{:S(2)}) async-start(), calls=%async_computation.3 | async-start | bytes 3145728 | tf_op jit(solution)/shard_map/psum | solution.py:265
  155.0 3.6 copy-start.14
  162.8 5.0 copy-start.15
  171.8 184.5 %all-reduce.14.cloned.1.call-start = ((), (), s32[]{:S(2)}) async-start(), calls=%async_computation.5 | async-start | bytes 6291456 | tf_op jit(solution)/shard_map/psum | solution.py:258
  251.2 3.3 copy-start.8
  251.2 3.8 copy-start.9
  251.2 7.0 %slice-start = ((s8[4718592]{0:T(1024)(128)(4,1)}), s8[4194304]{0:T(1024)(128)(4,1)S(1)}, s32[]{:S(2)}) async-start(s8[4718592]{0:T(1024)(128)(4,1)} %bitcast.76), calls=%async_computation.6 | async-start | bytes 8388608
  254.9 3.3 slice-start.1
  266.0 4.1 copy-start.28
  266.0 245.7 %all-reduce.12.cloned.1.call-start = ((), (), s32[]{:S(2)}) async-start(), calls=%async_computation.4 | async-start | bytes 8388608 | tf_op jit(solution)/shard_map/psum | solution.py:295
  266.3 3.8 copy-start.13
  272.0 3.5 copy-start.4
  275.5 4.0 copy-start.7
  275.5 4.0 copy-start.31
  511.6 4.6 copy-start.18
  514.6 3.2 copy-start.46
  514.6 4.0 copy-start.45
  516.2 3.2 copy-start.44
  516.2 4.1 copy-start.43
  516.2 4.9 copy-start.1
  (28 other events, 45.5 us)
Sparse Core Ops, SparseCore 0:
  9.7 43.0 all-gather.1
  65.4 86.8 all-reduce.7
  171.9 79.2 all-reduce.9
  266.1 90.1 all-reduce.13
  359.8 151.7 all-reduce.11
